TPU v7x, 32 devices: a whole 2x2x4 slice. The times are simulated.
32 devices in a mesh: row: 4 (over x, core), col: 8 (over z, y).
Axes of the slice: x: 2, y: 2, z: 4, core: 2. Of those that a mesh axis runs over, the one named last changes fastest.
Arguments:
- trailing: float32 [4096, 4096], P('row', 'col'), may hold values from -6 to 6
- panel_left: float32 [4096, 384], P(('row', 'col')), may hold values from -0.3125 to 0.3125
- panel_right: float32 [8, 1024, 384], P('row', 'col'), may hold values from -1 to 1
- panel_solved: float32 [1024, 1024], P('row', 'col'), may hold values from -1.75 to 1.75
- right_sides: float32 [4096, 1024], P('row', 'col'), may hold values from -6 to 6
- tile_ranks: int32 [8], replicated, may hold values from 64 to 384, as said below
- tile_order: int32 [8], replicated, may hold values from 0 to 7, each once
Outputs:
- trail_new: float32 [4096, 4096], P('row', 'col')
- rhs_new: float32 [4096, 1024], P('row', 'col')
Inputs may be any that keep to these rules, and one draw needn't show every extreme that they name: `tile_ranks`: every rank is a multiple of 64; both 64 and 384 occur in every draw. `tile_order`: each tile appears in exactly one slot.
All inputs are finite; a program needn't handle non-finite values.
Results may differ from a plain program's by a relative error of at most 0.00008.
Values sent between devices are 32-bit elements; how exact they have to be, the bound alone decides.
A program may use at most 64 MiB of HBM per device.

v0:
```python
import jax
import jax.numpy as jnp
from jax import lax
from jax.sharding import PartitionSpec as P


def spread(value, axis, root):
    mine = lax.axis_index(axis) == root
    return lax.psum(jnp.where(mine, value, jnp.zeros_like(value)), axis)


def exact_dot(left, right):
    return jnp.dot(left, right, precision=lax.Precision.HIGHEST, preferred_element_type=jnp.float32)


def on_device(trailing, panel_left, panel_right, panel_solved, right_sides, tile_ranks, tile_order):
    slot_count = panel_right.shape[0]
    tile_count = tile_order.shape[0]
    rank_width = panel_left.shape[1]
    left_rows, right_rows = (
        lax.all_gather(panel_left, "col", axis=0, tiled=True),
        lax.all_gather(panel_right, "col", axis=1, tiled=True),
    )
    tile_rows = left_rows.shape[0] // slot_count
    left_rows = left_rows.reshape(slot_count, tile_rows, rank_width)
    row_index = lax.axis_index("row")
    column = lax.axis_index("col")
    places = jnp.arange(tile_count, dtype=jnp.int32)
    levels = jnp.arange(rank_width, dtype=jnp.int32)
    slot_ids = row_index * slot_count + jnp.arange(slot_count, dtype=jnp.int32)
    my_tiles = jnp.sum(
        jnp.where(places[None, :] == slot_ids[:, None], tile_order[None, :], 0), axis=1
    )
    my_ranks = jnp.sum(
        jnp.where(places[None, :] == my_tiles[:, None], tile_ranks[None, :], 0), axis=1
    )
    keep_mask = (levels[None, :] < my_ranks[:, None]).astype(jnp.float32)
    left_mine = left_rows * keep_mask[:, None, :]
    root_slot = jnp.sum(jnp.where(tile_order == column, places, 0))
    root_row = root_slot // slot_count
    local_slot = root_slot % slot_count
    column_rank = jnp.sum(jnp.where(places == column, tile_ranks, 0))
    column_mask = (levels < column_rank).astype(jnp.float32)
    left_pick = (
        lax.dynamic_index_in_dim(left_rows, local_slot, 0, keepdims=False) * column_mask[None, :]
    )
    right_pick = lax.dynamic_index_in_dim(right_rows, local_slot, 0, keepdims=False)

    def owner_panel():
        return exact_dot(right_pick, left_pick.T)

    def other_panel():
        return jnp.zeros((right_pick.shape[0], tile_rows), jnp.float32)

    column_dense = lax.cond(row_index == root_row, owner_panel, other_panel)
    column_dense = spread(column_dense, "row", root_row)
    solved = jnp.einsum(
        "snk,nj->skj",
        right_rows,
        lax.all_gather(panel_solved, "row", axis=0, tiled=True),
        precision=lax.Precision.HIGHEST,
        preferred_element_type=jnp.float32,
    )
    updates = []
    for slot in range(slot_count):
        left_part = left_mine[slot]
        slot_right_part = right_rows[slot]
        middle = exact_dot(slot_right_part.T, column_dense)
        updates.append(exact_dot(left_part, jnp.concatenate([middle, solved[slot]], 1)))
    update_all = jnp.concatenate(updates, 0)
    trail_new = trailing - update_all[:, :tile_rows]
    rhs_new = right_sides - update_all[:, tile_rows:]
    return (trail_new, rhs_new)


def solution(mesh):
    return jax.shard_map(
        on_device,
        mesh=mesh,
        in_specs=(
            P("row", "col"),
            P(("row", "col"), None),
            P("row", "col", None),
            P("row", "col"),
            P("row", "col"),
            P(),
            P(),
        ),
        out_specs=(P("row", "col"), P("row", "col")),
        check_vma=False,
    )
```

profile of v0, /device:TPU:0, one launch (start us, length us, event | category | flops | bytes accessed | tf_op | source)
XLA Modules:
  0.0 198.6 jit_solution(3108771299947774375)
XLA Ops:
  7.2 0.0 all-gather.3.cloned.1.call-start
  7.2 0.7 all-gather.3.cloned.1.call-update
  7.9 0.0 all-gather.5.cloned.1.call-start
  7.9 0.7 all-gather.5.cloned.1.call-update
  8.6 0.0 all-reduce.2.cloned.1.call-start
  8.7 1.3 fusion.27
  12.6 1.0 copy.10
  13.6 1.3 fusion.28
  14.9 0.6 compare_convert_fusion
  15.6 0.8 fusion.25
  16.4 0.8 fusion.26
  17.2 0.1 compare_convert_fusion.1
  17.3 39.8 %all-gather.3.cloned.1.call-done = f32[1024,384]{1,0:T(8,128)} async-done(((f32[128,384]{1,0:T(8,128)}), f32[1024,384]{1,0:T(8,128)}) %all-gather.3.cloned.1.call-update) | async-done | bytes 1572880 | tf_op jit(solution)/shard_map/all_gather | solution.py:21
  57.1 60.6 %all-gather.5.cloned.1.call-done = f32[2,1024,384]{2,1,0:T(8,128)} async-done(((f32[2,128,384]{2,1,0:T(8,128)}), f32[2,1024,384]{2,1,0:T(8,128)}) %all-gather.5.cloned.1.call-update) | async-done | bytes 3145744 | tf_op jit(solution)/shard_map/all_gather | solution.py:22
  117.7 0.3 conditional.1
  117.7 0.2 broadcast.35
  118.0 1.5 broadcast_select_fusion
  119.5 0.0 all-reduce.2.cloned.1.call-update
  119.5 0.0 copy-start
  119.5 12.9 %all_gather.11 = f32[1024,128]{0,1:T(8,128)S(1)} all-gather(f32[256,128]{0,1:T(8,128)S(1)} %copy.10), channel_id=1, replica_groups=mesh['row'=4,'col'=8] {'row'}, dimensions={0}, use_global_device_ids=true | all-gather | bytes 655360 | tf_op jit(solution)/shard_map/all_gather | solution.py:60
  132.4 2.7 %broadcast_multiply_fusion = f32[2,512,384]{2,1,0:T(8,128)} fusion(f32[2,512,384]{2,1,0:T(8,128)} %bitcast.38, f32[2,384]{1,0:T(2,128)S(1)} %compare_convert_fusion.1), kind=kLoop, calls=%fused_computation.29 | loop fusion | flops 393216 | bytes 3148800 | tf_op jit(solution)/shard_map/mul | solution.py:38
  135.1 1.9 fusion.23
  137.1 37.4 %all-reduce.2.cloned.1.call-done = f32[1024,512]{1,0:T(8,128)} async-done(((f32[1024,512]{1,0:T(8,128)}), f32[1024,512]{1,0:T(8,128)}) %all-reduce.2.cloned.1.call-update) | async-done | bytes 2097168 | tf_op jit(solution)/shard_map/psum | solution.py:9
  174.5 5.2 %fusion.13 = f32[384,512]{0,1:T(8,128)S(1)} fusion(f32[1024,512]{1,0:T(8,128)} %all-reduce.2.cloned.1.call-done, f32[2,1024,384]{2,1,0:T(8,128)S(1)} %copy-done), kind=kOutput, calls=%fused_computation.17 | convolution fusion | flops 2415919104 | bytes 4456448 | tf_op jit(solution)/shard_map/dot_general | solution.py:13
  179.7 2.5 %fusion.18 = f32[512,640]{1,0:T(8,128)S(1)} fusion(f32[384,128]{0,1:T(8,128)S(1)} %get-tuple-element.85, f32[384,512]{0,1:T(8,128)S(1)} %fusion.13, f32[2,512,384]{2,1,0:T(8,128)S(1)} %copy-done.2), kind=kOutput, calls=%fused_computation.23 | convolution fusion | flops 1510195200 | bytes 3080192 | tf_op jit(solution)/shard_map/dot_general | solution.py:13
  182.3 3.8 %fusion.12 = f32[384,512]{0,1:T(8,128)S(1)} fusion(f32[1024,512]{1,0:T(8,128)S(1)} %copy-done.1, f32[2,1024,384]{2,1,0:T(8,128)S(1)} %copy-done), kind=kOutput, calls=%fused_computation.16 | convolution fusion | flops 2415919104 | bytes 4456448 | tf_op jit(solution)/shard_map/dot_general | solution.py:13
  186.1 0.0 copy-start.4
  186.1 2.5 %fusion.14 = f32[512,640]{1,0:T(8,128)S(1)} fusion(f32[384,128]{0,1:T(8,128)S(1)} %get-tuple-element.86, f32[384,512]{0,1:T(8,128)S(1)} %fusion.12, f32[2,512,384]{2,1,0:T(8,128)S(1)} %copy-done.2), kind=kOutput, calls=%fused_computation.19 | convolution fusion | flops 1510195200 | bytes 3080192 | tf_op jit(solution)/shard_map/dot_general | solution.py:13
  188.6 0.0 copy-start.3
  188.6 0.9 fusion.22
  189.5 0.9 copy-done.3
  190.4 1.6 fusion.9
  (8 shorter events, 0.0 us)
Async XLA Ops:
  7.2 49.9 %all-gather.3.cloned.1.call-start = ((), (), s32[]{:S(2)}) async-start(), calls=%async_computation | async-start | bytes 1769472 | tf_op jit(solution)/shard_map/all_gather | solution.py:21
  7.9 109.8 %all-gather.5.cloned.1.call-start = ((), (), s32[]{:S(2)}) async-start(), calls=%async_computation.1 | async-start | bytes 3538944 | tf_op jit(solution)/shard_map/all_gather | solution.py:22
  8.6 165.9 %all-reduce.2.cloned.1.call-start = ((), (), s32[]{:S(2)}) async-start(), calls=%async_computation.2 | async-start | bytes 4194304 | tf_op jit(solution)/shard_map/psum | solution.py:9
  119.5 15.6 %copy-start = (f32[2,1024,384]{2,1,0:T(8,128)S(1)}, f32[2,1024,384]{2,1,0:T(8,128)}, u32[]{:S(2)}) copy-start(f32[2,1024,384]{2,1,0:T(8,128)} %all-gather.5.cloned.1.call-done) | copy-start | bytes 9437188
  174.5 5.2 %copy-start.2 = (f32[2,512,384]{2,1,0:T(8,128)S(1)}, f32[2,512,384]{2,1,0:T(8,128)}, u32[]{:S(2)}) copy-start(f32[2,512,384]{2,1,0:T(8,128)} %broadcast_multiply_fusion) | copy-start | bytes 4718596
  179.7 2.5 %copy-start.1 = (f32[1024,512]{1,0:T(8,128)S(1)}, f32[1024,512]{1,0:T(8,128)}, u32[]{:S(2)}) copy-start(f32[1024,512]{1,0:T(8,128)} %all-reduce.2.cloned.1.call-done) | copy-start | bytes 6291460
  186.1 2.5 %copy-start.4 = (f32[1024,128]{1,0:T(8,128)S(1)}, f32[1024,128]{1,0:T(8,128)}, u32[]{:S(2)}) copy-start(f32[1024,128]{1,0:T(8,128)} %param.13) | copy-start | bytes 1572868
  188.6 1.8 copy-start.3
Sparse Core Ops, SparseCore 0:
  10.2 46.8 all-gather.2
  59.3 58.3 all-gather.4
  120.6 53.8 all-reduce.1
where the time goes:
time: 199 us
  waiting for transfers between devices  139 us (70%)
  between operations  16.5 us (8%)
  matrix products  16 us (8%)
  blocking collectives  12.9 us (6%)
  other arithmetic  11.7 us (6%)
  local copies, waits for them, and re-layouts  2.21 us (1%)
    all_gather x1, waiting for transfers between devices, on_device(): lax.all_gather(panel_right, 'col', axis=1, tiled=True)  60.6 us
    all_gather x1, waiting for transfers between devices, on_device(): lax.all_gather(panel_left, 'col', axis=0, tiled=True)  39.8 us
    psum x1, waiting for transfers between devices, spread(): return lax.psum(jnp.where(mine, value, jnp.zeros_like(value)), axis)  37.4 us
    dot_general x4, matrix products, exact_dot(): jnp.dot(left, right, precision=lax.Precision.HIGHEST, preferred_element_t...  14 us
    all_gather x1, blocking collectives, on_device(): lax.all_gather(panel_solved, 'row', axis=0, tiled=True)  12.9 us
  transfers between devices with their start and end apart: 3, of which 3 were waited for; matrix products, arithmetic and copies ran while one was open for 5% of the time, Pallas kernels for 0%

commit v1 on v0

v1 whole, which is shorter than its diff:
```python
import functools

import jax
import jax.numpy as jnp
from jax import lax
from jax.experimental import pallas as pl
from jax.experimental.pallas import tpu as pltpu
from jax.sharding import PartitionSpec as P

MESH = pl.DeviceIdType.MESH
ACROSS = 2
CORES = 2


def gather_kernel(n_row, n_col, slots, place, left, right, solved, rows_l, rows_r, tile, rows_w,
                  first_out, first_in, chip, far_in, own_sem, rsem, zsem, ysem, fsem, frsem, xsem, xrsem, tsem, trsem, wsem, wrsem):
    length = n_col // ACROSS
    half = length // slots
    teams = n_row // CORES
    row, col = lax.axis_index("row"), lax.axis_index("col")
    z, y = col // ACROSS, col % ACROSS
    team, core = row // CORES, row % CORES
    pair = team * CORES + (1 - core)
    mate = z * ACROSS + (1 - y)

    barrier = pltpu.get_barrier_semaphore()

    def greet(r, c):
        pl.semaphore_signal(barrier, inc=1, device_id=(r, c), device_id_type=MESH)

    @pl.when(z > 0)
    def _():
        greet(row, col - ACROSS)

    @pl.when(z < length - 1)
    def _():
        greet(row, col + ACROSS)

    greet(row, mate)
    for k in range(1, n_row):
        greet(lax.rem(row + k, n_row), col)

    def piece(p, c):
        return rows_l.at[c] if p == 0 else rows_r.at[p - 1, c]

    own = [pltpu.make_async_copy(left, piece(0, col), own_sem.at[0])]
    for s in range(slots):
        own.append(pltpu.make_async_copy(right.at[s], piece(s + 1, col), own_sem.at[s + 1]))
    own.append(pltpu.make_async_copy(solved, rows_w.at[row], own_sem.at[slots + 1]))
    for copy in own:
        copy.start()
    for copy in own:
        copy.wait()
    pl.semaphore_wait(barrier, (z > 0).astype(jnp.int32) + (z < length - 1).astype(jnp.int32) + n_row)

    def z_copy(p, src, way):
        c = src * ACROSS + y
        to = col + (ACROSS if way == 0 else -ACROSS)
        return pltpu.make_async_remote_copy(piece(p, c), piece(p, c), zsem.at[way, p, src], rsem.at[p, c], device_id=(row, to), device_id_type=MESH)

    def y_copy(p, src, c):
        return pltpu.make_async_remote_copy(piece(p, c), piece(p, c), ysem.at[p, src], rsem.at[p, c], device_id=(row, mate), device_id_type=MESH)

    def w_copy(k):
        return pltpu.make_async_remote_copy(rows_w.at[row], rows_w.at[row], wsem.at[k], wrsem.at[row], device_id=(lax.rem(row + k, n_row), col), device_id_type=MESH)

    def f_copy(i):
        return pltpu.make_async_remote_copy(first_out.at[i], first_in.at[i], fsem.at[i], frsem.at[i], device_id=(pair, col), device_id_type=MESH)

    def x_copy(i, k, source):
        to = lax.rem(team + k, teams)
        return pltpu.make_async_remote_copy(chip.at[i], far_in.at[source, i], xsem.at[k, i], xrsem.at[source, i], device_id=(to * CORES + core, col), device_id_type=MESH)

    def t_copy(i, c):
        return pltpu.make_async_remote_copy(tile.at[c], tile.at[c], tsem.at[i], trsem.at[c], device_id=(pair, col), device_id_type=MESH)

    for k in range(1, n_row):
        w_copy(k).start()

    root_slot = place[0]
    local = lax.rem(root_slot, slots)
    root_row = root_slot // slots
    root_team = root_row // CORES

    def candidate(i, which, is_left):
        parts = []
        for s in range(slots):
            if is_left:
                parts.append(rows_l[((i - length) + s * half) * ACROSS + which])
            else:
                parts.append(rows_r[s, i * ACROSS + which])
        value = parts[0]
        for s in range(1, slots):
            value = jnp.where(local == s, parts[s], value)
        return value

    def stage_one(i, is_left):
        first_out[i] = candidate(i, 1 - core, is_left)
        f_copy(i).start()

    def stage_two(i, is_left):
        mine = candidate(i, core, is_left)
        f_copy(i).wait_recv()
        chip[i] = jnp.where(root_row == row, mine, first_in[i])
        for k in range(1, teams):
            x_copy(i, k, team).start()

    def stage_three(i, is_left):
        value = chip[i]
        for k in range(1, teams):
            other = lax.rem(team + k, teams)
            x_copy(i, k, other).wait_recv()
            value = jnp.where(root_team == other, far_in[other, i], value)
        c = i * ACROSS + core
        tile[c] = value
        t_copy(i, c).start()

    def sources(d, body):
        for side in range(2):
            src = z - d if side == 0 else z + d
            ok = src >= 0 if side == 0 else (src < length) & (d > 0)
            pl.when(ok)(functools.partial(body, src, side))

    def ready(d, body):
        def lefts(q, _):
            last = jnp.maximum(jnp.abs(z - q), jnp.abs(z - q - half))
            for s in range(1, slots):
                last = jnp.maximum(last, jnp.abs(z - q - s * half))

            @pl.when(last == d)
            def _():
                body(length + q, True)

            return 0

        lax.fori_loop(0, half, lefts, 0)
        sources(d, lambda src, side: body(src, False))

    def forward(d):
        for p in range(slots + 1):
            def one(src, side, p=p):
                @pl.when(d > 0)
                def _():
                    y_copy(p, src, src * ACROSS + y).wait_recv()

                @pl.when((z < length - 1) & ((side == 0) | (d == 0)))
                def _():
                    z_copy(p, src, 0).start()

                @pl.when((z > 0) & ((side == 1) | (d == 0)))
                def _():
                    z_copy(p, src, 1).start()

                y_copy(p, src, src * ACROSS + y).start()

            sources(d, one)

    def arrive(d):
        def one(src, side):
            for p in range(slots + 1):
                y_copy(p, src, src * ACROSS + 1 - y).wait_recv()

        sources(d, one)

    def step(d, _):
        @pl.when(d < length)
        def _():
            forward(d)

        @pl.when((d >= 1) & (d <= length))
        def _():
            arrive(d - 1)
            ready(d - 1, stage_one)
            ready(d - 1, stage_two)

        @pl.when(d >= 2)
        def _():
            ready(d - 2, stage_three)

        return 0

    lax.fori_loop(0, length + 2, step, 0)

    def drain(d, _):
        for p in range(slots + 1):
            def one(src, side, p=p):
                @pl.when((z < length - 1) & ((side == 0) | (d == 0)))
                def _():
                    z_copy(p, src, 0).wait_send()

                @pl.when((z > 0) & ((side == 1) | (d == 0)))
                def _():
                    z_copy(p, src, 1).wait_send()

                y_copy(p, src, src * ACROSS + y).wait_send()

            sources(d, one)
        return 0

    lax.fori_loop(0, length, drain, 0)

    def finish(i, _):
        f_copy(i).wait_send()
        for k in range(1, teams):
            x_copy(i, k, team).wait_send()
        t_copy(i, i * ACROSS + core).wait_send()
        t_copy(i, i * ACROSS + 1 - core).wait_recv()
        return 0

    lax.fori_loop(0, length + half, finish, 0)
    for k in range(1, n_row):
        w_copy(k).wait_send()
        other = lax.rem(row + k, n_row)
        pltpu.make_async_remote_copy(rows_w.at[other], rows_w.at[other], wsem.at[k], wrsem.at[other], device_id=(other, col), device_id_type=MESH).wait_recv()


def gather(n_row, n_col, place, left, right, solved):
    slots, depth, width = right.shape
    length = n_col // ACROSS
    half = length // slots
    teams = n_row // CORES
    chunks = length + half
    f32 = jnp.float32
    block = (depth, width)
    vmem = pl.BlockSpec(memory_space=pltpu.VMEM)
    dma = pltpu.SemaphoreType.DMA
    return pl.pallas_call(
        functools.partial(gather_kernel, n_row, n_col, slots),
        out_shape=(
            jax.ShapeDtypeStruct((n_col,) + left.shape, f32),
            jax.ShapeDtypeStruct((slots, n_col) + block, f32),
            jax.ShapeDtypeStruct((chunks * ACROSS,) + block, f32),
            jax.ShapeDtypeStruct((n_row,) + solved.shape, f32),
        ),
        in_specs=[pl.BlockSpec(memory_space=pltpu.SMEM), vmem, vmem, vmem],
        out_specs=(vmem, vmem, vmem, vmem),
        scratch_shapes=[
            pltpu.VMEM((chunks,) + block, f32),
            pltpu.VMEM((chunks,) + block, f32),
            pltpu.VMEM((chunks,) + block, f32),
            pltpu.VMEM((teams, chunks) + block, f32),
            dma((slots + 2,)),
            dma((slots + 1, n_col)),
            dma((2, slots + 1, length)),
            dma((slots + 1, length)),
            dma((chunks,)),
            dma((chunks,)),
            dma((teams, chunks)),
            dma((teams, chunks)),
            dma((chunks,)),
            dma((chunks * ACROSS,)),
            dma((n_row,)),
            dma((n_row,)),
        ],
        compiler_params=pltpu.CompilerParams(collective_id=0, has_side_effects=True, vmem_limit_bytes=48 * 1024 * 1024),
        name="gather_panel",
    )(place, left, right, solved)


def high(spec, a, b):
    return jnp.einsum(spec, a, b, precision=lax.Precision.HIGH, preferred_element_type=jnp.float32)


def on_device(n_row, n_col, trailing, panel_left, panel_right, panel_solved, right_sides, tile_ranks, tile_order):
    slots, _, width = panel_right.shape
    count = tile_order.shape[0]
    row, column = lax.axis_index("row"), lax.axis_index("col")
    places = jnp.arange(count, dtype=jnp.int32)
    levels = jnp.arange(width, dtype=jnp.int32)
    root = jnp.sum(jnp.where(tile_order == column, places, 0)).astype(jnp.int32)
    rows_l, rows_r, tile, rows_w = gather(n_row, n_col, root[None], panel_left, panel_right, panel_solved)
    slot_ids = row * slots + jnp.arange(slots, dtype=jnp.int32)
    my_tiles = jnp.sum(jnp.where(places[None, :] == slot_ids[:, None], tile_order[None, :], 0), axis=1)
    my_ranks = jnp.sum(jnp.where(places[None, :] == my_tiles[:, None], tile_ranks[None, :], 0), axis=1)
    column_rank = jnp.sum(jnp.where(places == column, tile_ranks, 0))
    left = rows_l.reshape(slots, -1, width)
    left = jnp.where(levels[None, None, :] < my_ranks[:, None, None], left, 0.0)
    right = rows_r.reshape(slots, -1, width)
    tile_right = tile[:n_col].reshape(-1, width)
    tile_left = tile[n_col:].reshape(-1, width)
    tile_left = jnp.where(levels[None, :] < column_rank, tile_left, 0.0)
    solved = rows_w.reshape(-1, rows_w.shape[-1])
    both = high("sjk,jm->skm", right, jnp.concatenate([tile_right, solved], 1))
    middle = high("skm,im->ski", both[:, :, :width], tile_left)
    update = high("sik,skn->sin", left, jnp.concatenate([middle, both[:, :, width:]], 2))
    tile_rows = tile_left.shape[0]
    update = update.reshape(slots * tile_rows, -1)
    return trailing - update[:, :tile_rows], right_sides - update[:, tile_rows:]


def solution(mesh):
    return jax.shard_map(
        functools.partial(on_device, mesh.shape["row"], mesh.shape["col"]),
        mesh=mesh,
        in_specs=(
            P("row", "col"),
            P(("row", "col"), None),
            P("row", "col", None),
            P("row", "col"),
            P("row", "col"),
            P(),
            P(),
        ),
        out_specs=(P("row", "col"), P("row", "col")),
        check_vma=False,
    )
```

time: 199 us -> 90.3 us (0.45)
  waiting for transfers between devices: 139 us -> 0 us
  Pallas kernels: 0 us -> 71.4 us
  between operations: 16.5 us -> 0.76 us
  blocking collectives: 12.9 us -> 0 us
  matrix products: 16 us -> 6.77 us
  other arithmetic: 11.7 us -> 6.35 us
  local copies, waits for them, and re-layouts: 2.21 us -> 4.75 us
    all_gather x2 -> x0, waiting for transfers between devices: 100 us -> none  [the longest x1 60.6 us: on_device(): lax.all_gather(panel_right, 'col', axis=1, tiled=True)]
    pallas_call x0 -> x1, Pallas kernels: none -> 71.4 us  [gather(): pl.pallas_call(functools.partial(gather_kernel, n_row, n_col, slots), out...]
    psum x1 -> x0, waiting for transfers between devices: 37.4 us -> none  [spread(): return lax.psum(jnp.where(mine, value, jnp.zeros_like(value)), axis)]
    all_gather x1 -> x0, blocking collectives: 12.9 us -> none  [on_device(): lax.all_gather(panel_solved, 'row', axis=0, tiled=True)]
    dot_general x5 -> x3, matrix products: 16 us -> 6.77 us  [high(): jnp.einsum(spec, a, b, precision=lax.Precision.HIGH, preferred_element_ty...]
    mul x1 -> x0, other arithmetic: 2.66 us -> none  [on_device(): left_mine = left_rows * keep_mask[:, None, :]]
    unnamed x11 -> x12, local copies, waits for them, and re-layouts: 1.93 us -> 4.54 us
  transfers between devices with their start and end apart: 3 -> 0, of which waited for: 3 -> 0; matrix products, arithmetic and copies ran while one was open for 5% -> 0% of each run, Pallas kernels for 0% -> 0%
where the time goes in v1:
time: 90.3 us; the launch traced here: 90 us
  Pallas kernels  71.4 us (79%)
  matrix products  6.77 us (7%)
  other arithmetic  6.35 us (7%)
  local copies, waits for them, and re-layouts  4.75 us (5%)
    pallas_call x1, Pallas kernels, gather(): pl.pallas_call(functools.partial(gather_kernel, n_row, n_col, slots), out...  71.4 us
    dot_general x3, matrix products, high(): jnp.einsum(spec, a, b, precision=lax.Precision.HIGH, preferred_element_ty...  6.77 us
    unnamed x12, local copies, waits for them, and re-layouts  4.54 us

profile of v1, /device:TPU:0, one launch (start us, length us, event | category | flops | bytes accessed | tf_op | source)
XLA Modules:
  0.0 90.0 jit_solution(14872245417589213695)
XLA Ops:
  0.6 0.8 fusion.10
  1.5 0.8 fusion.11
  2.3 1.3 %fusion.12 = (s32[]{:T(128)}, s32[]{:T(128)}) fusion(s32[8]{0:T(128)} %param.13, s32[]{:T(128)S(6)} %axis_index.25, s32[8]{0:T(128)} %param.12), kind=kLoop, calls=%fused_computation.23 | loop fusion | flops 46 | bytes 76 | tf_op jit(solution)/shard_map/reduce_sum | solution.py:270
  3.6 0.6 iota_compare_fusion.1
  4.3 0.1 iota_compare_fusion
  4.4 0.0 copy-start
  4.4 1.0 %copy-done = f32[2,128,384]{2,1,0:T(8,128)S(1)} copy-done((f32[2,128,384]{2,1,0:T(8,128)S(1)}, f32[2,128,384]{2,1,0:T(8,128)}, u32[]{:S(2)}) %copy-start) | copy-done | bytes 393240
  5.4 0.0 copy-start.1
  5.4 0.9 %copy-done.1 = f32[128,384]{1,0:T(8,128)S(1)} copy-done((f32[128,384]{1,0:T(8,128)S(1)}, f32[128,384]{1,0:T(8,128)}, u32[]{:S(2)}) %copy-start.1) | copy-done | bytes 196632
  6.3 0.0 copy-start.2
  6.3 0.9 %copy-done.2 = f32[256,128]{1,0:T(8,128)S(1)} copy-done((f32[256,128]{1,0:T(8,128)S(1)}, f32[256,128]{1,0:T(8,128)}, u32[]{:S(2)}) %copy-start.2) | copy-done | bytes 131096
  7.2 71.4 %gather_panel.1 = (f32[8,128,384]{2,1,0:T(8,128)S(1)}, f32[2,8,128,384]{3,2,1,0:T(8,128)}, f32[12,128,384]{2,1,0:T(8,128)S(1)}, f32[4,256,128]{2,1,0:T(8,128)S(1)}) custom-call(s32[1]{0:T(128)} %bitcast.place, f32[128,384]{1,0:T(8,128)S(1)} %copy-done.1, f32[2,128,384]{2,1,0:T(8,128)S(1)} %copy-done, f32[256,128]{1,0:T(8,128)S(1)} %copy-done.2), custom_call_target="tpu_custom_call" | custom-call | tf_op jit(solution)/shard_map/gather_panel/pallas_call | solution.py:227
  78.6 0.1 bitcast_select_fusion
  78.7 0.1 slice.20
  78.8 0.0 copy-start.3
  78.8 0.1 slice.18
  78.9 0.1 bitcast_select_fusion.1
  79.0 1.7 %copy-done.3 = f32[2,8,128,384]{3,2,1,0:T(8,128)S(1)} copy-done((f32[2,8,128,384]{3,2,1,0:T(8,128)S(1)}, f32[2,8,128,384]{3,2,1,0:T(8,128)}, u32[]{:S(2)}) %copy-start.3) | copy-done | bytes 3145752
  80.7 2.7 %fusion = f32[2,384,512]{2,1,0:T(8,128)S(1)} fusion(f32[2,1024,384]{2,1,0:T(8,128)S(1)} %bitcast.23, f32[1024,128]{1,0:T(8,128)S(1)} %bitcast.19, f32[1024,384]{1,0:T(8,128)S(1)} %bitcast.22), kind=kOutput, calls=%fused_computation.2 | convolution fusion | flops 2416443392 | bytes 6815744 | tf_op jit(solution)/shard_map/sjk,jm->skm/dot_general | solution.py:261
  83.4 0.1 slice.25
  83.5 1.4 %fusion.7 = f32[2,384,512]{2,1,0:T(8,128)S(1)} fusion(f32[2,384,512]{2,1,0:T(8,128)S(1)} %fusion, f32[512,384]{1,0:T(8,128)S(1)} %bitcast_select_fusion.1), kind=kOutput, calls=%fused_computation.10 | convolution fusion | flops 905969664 | bytes 3538944 | tf_op jit(solution)/shard_map/skm,im->ski/dot_general | solution.py:261
  84.9 0.0 copy-start.5
  84.9 0.0 copy-start.4
  84.9 2.6 %fusion.3 = f32[2,512,640]{2,1,0:T(8,128)S(1)} fusion(f32[2,512,384]{2,1,0:T(8,128)S(1)} %bitcast_select_fusion, f32[2,384,128]{2,1,0:T(8,128)S(1)} %slice.25, f32[2,384,512]{2,1,0:T(8,128)S(1)} %fusion.7), kind=kOutput, calls=%fused_computation.5 | convolution fusion | flops 1510440960 | bytes 6160384 | tf_op jit(solution)/shard_map/sik,skn->sin/dot_general | solution.py:261
  87.5 0.0 copy-done.5
  87.6 0.8 slice_subtract_fusion.1
  88.4 0.0 copy-done.4
  88.4 1.6 %slice_subtract_fusion = f32[1024,512]{1,0:T(8,128)} fusion(f32[1024,512]{1,0:T(8,128)S(1)} %copy-done.4, f32[1024,640]{1,0:T(8,128)S(1)} %bitcast.21), kind=kLoop, calls=%fused_computation | loop fusion | flops 524288 | bytes 6291456 | tf_op jit(solution)/shard_map/sub | solution.py:288
  (1 shorter events, 0.0 us)
Async XLA Ops:
  4.4 1.0 %copy-start = (f32[2,128,384]{2,1,0:T(8,128)S(1)}, f32[2,128,384]{2,1,0:T(8,128)}, u32[]{:S(2)}) copy-start(f32[2,128,384]{2,1,0:T(8,128)} %right.1) | copy-start | bytes 1179652
  5.4 0.9 %copy-start.1 = (f32[128,384]{1,0:T(8,128)S(1)}, f32[128,384]{1,0:T(8,128)}, u32[]{:S(2)}) copy-start(f32[128,384]{1,0:T(8,128)} %left.1) | copy-start | bytes 589828
  6.3 0.9 %copy-start.2 = (f32[256,128]{1,0:T(8,128)S(1)}, f32[256,128]{1,0:T(8,128)}, u32[]{:S(2)}) copy-start(f32[256,128]{1,0:T(8,128)} %solved.1) | copy-start | bytes 393220
  78.8 1.9 %copy-start.3 = (f32[2,8,128,384]{3,2,1,0:T(8,128)S(1)}, f32[2,8,128,384]{3,2,1,0:T(8,128)}, u32[]{:S(2)}) copy-start(f32[2,8,128,384]{3,2,1,0:T(8,128)} %get-tuple-element.7) | copy-start | bytes 9437188
  84.9 2.6 %copy-start.5 = (f32[1024,128]{1,0:T(8,128)S(1)}, f32[1024,128]{1,0:T(8,128)}, u32[]{:S(2)}) copy-start(f32[1024,128]{1,0:T(8,128)} %param.11) | copy-start | bytes 1572868
  84.9 3.5 %copy-start.4 = (f32[1024,512]{1,0:T(8,128)S(1)}, f32[1024,512]{1,0:T(8,128)}, u32[]{:S(2)}) copy-start(f32[1024,512]{1,0:T(8,128)} %param.7) | copy-start | bytes 6291460

commit v2 on v1

v2 whole, which is shorter than its diff:
```python
import functools

import jax
import jax.numpy as jnp
from jax import lax
from jax.experimental import pallas as pl
from jax.experimental.pallas import tpu as pltpu
from jax.sharding import PartitionSpec as P

MESH = pl.DeviceIdType.MESH
ACROSS = 2
CORES = 2


def sides(z, length, d, body):
    for side in range(2):
        src = z - d if side == 0 else z + d
        ok = src >= 0 if side == 0 else (src < length) & (d > 0)
        pl.when(ok)(functools.partial(body, src, side))


def find(order, value):
    place = jnp.int32(0)
    for i in range(order.shape[0]):
        place = jnp.where(order[i] == value, jnp.int32(i), place)
    return place


def gather_kernel(n_row, n_col, slots, order, left, right, solved, rows_l, rows_r, tile, rows_w,
                  first_out, first_in, chip, far_in, own_sem, rsem, zsem, ysem, fsem, frsem, xsem, xrsem, tsem, trsem, wsem, wrsem):
    length = n_col // ACROSS
    half = length // slots
    teams = n_row // CORES
    part = tile.shape[1] // CORES
    late = slots + 1
    row, col = lax.axis_index("row"), lax.axis_index("col")
    z, y = col // ACROSS, col % ACROSS
    team, core = row // CORES, row % CORES
    pair = team * CORES + (1 - core)
    mate = z * ACROSS + (1 - y)

    barrier = pltpu.get_barrier_semaphore()

    def greet(r, c):
        pl.semaphore_signal(barrier, inc=1, device_id=(r, c), device_id_type=MESH)

    @pl.when(z > 0)
    def _():
        greet(row, col - ACROSS)

    @pl.when(z < length - 1)
    def _():
        greet(row, col + ACROSS)

    greet(row, mate)
    for k in range(1, n_row):
        greet(lax.rem(row + k, n_row), col)

    cut = left.shape[0] // 2

    def piece(p, c):
        if p == 0:
            return rows_l.at[c, pl.ds(0, cut)]
        if p == late:
            return rows_l.at[c, pl.ds(cut, cut)]
        return rows_r.at[p - 1, c]

    own = [pltpu.make_async_copy(left, rows_l.at[col], own_sem.at[0])]
    for s in range(slots):
        own.append(pltpu.make_async_copy(right.at[s], piece(s + 1, col), own_sem.at[s + 1]))
    own.append(pltpu.make_async_copy(solved, rows_w.at[row], own_sem.at[slots + 1]))
    for copy in own:
        copy.start()
    for copy in own:
        copy.wait()
    pl.semaphore_wait(barrier, (z > 0).astype(jnp.int32) + (z < length - 1).astype(jnp.int32) + n_row)

    def z_copy(p, src, way, across=None):
        c = src * ACROSS + (y if across is None else across)
        lane = p if across is None else late + 1
        to = col + (ACROSS if way == 0 else -ACROSS)
        return pltpu.make_async_remote_copy(piece(p, c), piece(p, c), zsem.at[way, lane, src], rsem.at[p, c], device_id=(row, to), device_id_type=MESH)

    def y_copy(p, src, c):
        return pltpu.make_async_remote_copy(piece(p, c), piece(p, c), ysem.at[p, src], rsem.at[p, c], device_id=(row, mate), device_id_type=MESH)

    def w_copy(k):
        return pltpu.make_async_remote_copy(rows_w.at[row], rows_w.at[row], wsem.at[k], wrsem.at[row], device_id=(lax.rem(row + k, n_row), col), device_id_type=MESH)

    def f_copy(c):
        return pltpu.make_async_remote_copy(first_out.at[c], first_in.at[c], fsem.at[c], frsem.at[c], device_id=(pair, col), device_id_type=MESH)

    def x_copy(c, k, source):
        to = lax.rem(team + k, teams)
        return pltpu.make_async_remote_copy(chip.at[c], far_in.at[source, c], xsem.at[k, c], xrsem.at[source, c], device_id=(to * CORES + core, col), device_id_type=MESH)

    def rows_of(which):
        return pl.ds(pl.multiple_of(which * part, part), part)

    def t_copy(c, which):
        ref = tile.at[c, rows_of(which)]
        return pltpu.make_async_remote_copy(ref, ref, tsem.at[c], trsem.at[c], device_id=(pair, col), device_id_type=MESH)

    root_slot = find(order, col)
    local = lax.rem(root_slot, slots)
    root_row = root_slot // slots
    root_team = root_row // CORES

    def candidate(c, which, is_left):
        parts = []
        for s in range(slots):
            if is_left:
                parts.append(rows_l[(c - n_col) + s * (n_col // slots), rows_of(which)])
            else:
                parts.append(rows_r[s, c, rows_of(which)])
        value = parts[0]
        for s in range(1, slots):
            value = jnp.where(local == s, parts[s], value)
        return value

    def stage_one(c, is_left):
        first_out[c] = candidate(c, 1 - core, is_left)
        f_copy(c).start()

    def stage_two(c, is_left):
        mine = candidate(c, core, is_left)
        f_copy(c).wait_recv()
        chip[c] = jnp.where(root_row == row, mine, first_in[c])
        for k in range(1, teams):
            x_copy(c, k, team).start()

    def stage_three(c, is_left):
        value = chip[c]
        for k in range(1, teams):
            other = lax.rem(team + k, teams)
            x_copy(c, k, other).wait_recv()
            value = jnp.where(root_team == other, far_in[other, c], value)
        tile[c, rows_of(core)] = value
        t_copy(c, core).start()

    def sources(d, body):
        sides(z, length, d, body)

    def near(d, body):
        sources(d, lambda src, side: body(src * ACROSS + y, False))

    def lefts(d, body):
        def one(q, _):
            last = jnp.abs(z - q)
            for s in range(1, slots):
                last = jnp.maximum(last, jnp.abs(z - q - s * half))

            @pl.when(last == d)
            def _():
                for across in range(ACROSS):
                    body(n_col + q * ACROSS + across, True)

            return 0

        lax.fori_loop(0, half, one, 0)

    def far(d, body):
        lefts(d, body)
        sources(d, lambda src, side: body(src * ACROSS + 1 - y, False))

    def along(d, side, act):
        @pl.when((z < length - 1) & ((side == 0) | (d == 0)))
        def _():
            act(0)

        @pl.when((z > 0) & ((side == 1) | (d == 0)))
        def _():
            act(1)

    def forward(d):
        for p in range(late):
            def one(src, side, p=p):
                @pl.when(d > 0)
                def _():
                    y_copy(p, src, src * ACROSS + y).wait_recv()

                y_copy(p, src, src * ACROSS + y).start()
                along(d, side, lambda way: z_copy(p, src, way).start())

            sources(d, one)

        def both(src, side):
            @pl.when(d > 0)
            def _():
                y_copy(late, src, src * ACROSS + y).wait_recv()

            @pl.when(d == 0)
            def _():
                y_copy(late, src, src * ACROSS + y).start()

            along(d, side, lambda way: z_copy(late, src, way).start())
            y_copy(late, src, src * ACROSS + 1 - y).wait_recv()
            along(d, side, lambda way: z_copy(late, src, way, 1 - y).start())

        sources(d, both)

    def arrive(d):
        def one(src, side):
            for p in range(late):
                y_copy(p, src, src * ACROSS + 1 - y).wait_recv()

        sources(d, one)

    def step(d, _):
        @pl.when(d < length)
        def _():
            forward(d)
            near(d, stage_one)

        @pl.when(d == 0)
        def _():
            for k in range(1, n_row):
                w_copy(k).start()

        @pl.when((d >= 1) & (d <= length))
        def _():
            arrive(d - 1)
            far(d - 1, stage_one)

        @pl.when(d < length)
        def _():
            near(d, stage_two)

        @pl.when((d >= 1) & (d <= length))
        def _():
            far(d - 1, stage_two)
            near(d - 1, stage_three)

        @pl.when(d >= 2)
        def _():
            far(d - 2, stage_three)

        return 0

    lax.fori_loop(0, length + 2, step, 0)

    def drain(d, _):
        def one(src, side):
            for p in range(late):
                y_copy(p, src, src * ACROSS + y).wait_send()
                along(d, side, lambda way: z_copy(p, src, way).wait_send())

            @pl.when(d == 0)
            def _():
                y_copy(late, src, src * ACROSS + y).wait_send()

            along(d, side, lambda way: z_copy(late, src, way).wait_send())
            along(d, side, lambda way: z_copy(late, src, way, 1 - y).wait_send())

        sources(d, one)
        return 0

    lax.fori_loop(0, length, drain, 0)

    def finish(c, _):
        f_copy(c).wait_send()
        for k in range(1, teams):
            x_copy(c, k, team).wait_send()
        t_copy(c, core).wait_send()
        t_copy(c, 1 - core).wait_recv()
        return 0

    lax.fori_loop(0, n_col + half * ACROSS, finish, 0)
    for k in range(1, n_row):
        w_copy(k).wait_send()
        other = lax.rem(row + k, n_row)
        pltpu.make_async_remote_copy(rows_w.at[other], rows_w.at[other], wsem.at[k], wrsem.at[other], device_id=(other, col), device_id_type=MESH).wait_recv()


def gather(n_row, n_col, order, left, right, solved):
    slots, depth, width = right.shape
    length = n_col // ACROSS
    teams = n_row // CORES
    chunks = n_col + n_col // slots
    f32 = jnp.float32
    block = (depth, width)
    part = (depth // CORES, width)
    vmem = pl.BlockSpec(memory_space=pltpu.VMEM)
    hbm = pl.BlockSpec(memory_space=pltpu.HBM)
    dma = pltpu.SemaphoreType.DMA
    return pl.pallas_call(
        functools.partial(gather_kernel, n_row, n_col, slots),
        out_shape=(
            jax.ShapeDtypeStruct((n_col,) + left.shape, f32),
            jax.ShapeDtypeStruct((slots, n_col) + block, f32),
            jax.ShapeDtypeStruct((chunks,) + block, f32),
            jax.ShapeDtypeStruct((n_row,) + solved.shape, f32),
        ),
        in_specs=[pl.BlockSpec(memory_space=pltpu.SMEM), hbm, hbm, hbm],
        out_specs=(vmem, vmem, vmem, vmem),
        scratch_shapes=[
            pltpu.VMEM((chunks,) + part, f32),
            pltpu.VMEM((chunks,) + part, f32),
            pltpu.VMEM((chunks,) + part, f32),
            pltpu.VMEM((teams, chunks) + part, f32),
            dma((slots + 2,)),
            dma((slots + 2, n_col)),
            dma((2, slots + 3, length)),
            dma((slots + 2, length)),
            dma((chunks,)),
            dma((chunks,)),
            dma((teams, chunks)),
            dma((teams, chunks)),
            dma((chunks,)),
            dma((chunks,)),
            dma((n_row,)),
            dma((n_row,)),
        ],
        compiler_params=pltpu.CompilerParams(collective_id=0, has_side_effects=True, vmem_limit_bytes=28 * 1024 * 1024),
        name="gather_panel",
    )(order, left, right, solved)


def cut_two(x):
    high = x.astype(jnp.bfloat16)
    return high, (x - high.astype(jnp.float32)).astype(jnp.bfloat16)


def dot3(a, b, dims):
    (ah, al), (bh, bl) = a, b

    def dot(u, v):
        return lax.dot_general(u, v, (dims, ((), ())), preferred_element_type=jnp.float32)

    return dot(ah, bh) + (dot(ah, bl) + dot(al, bh))


def update_kernel(order, ranks, rows_l, rows_r, tile, rows_w, trailing, sides_in, trail_out, rhs_out, mid_high, mid_low):
    slots = rows_r.shape[0]
    n_col, depth, width = tile.shape
    n_col = rows_r.shape[1]
    slot, step = pl.program_id(0), pl.program_id(1)

    @pl.when(step == 0)
    def _():
        tile_id = order[lax.axis_index("row") * slots + slot]
        rank = ranks[tile_id]
        column_rank = ranks[lax.axis_index("col")]
        lane = lax.broadcasted_iota(jnp.int32, (1, width), 1)
        sub = lax.broadcasted_iota(jnp.int32, (width, 1), 0)
        right = cut_two(rows_r[slot].reshape(n_col * depth, width))
        tile_right = cut_two(tile[:n_col].reshape(n_col * depth, width))
        solved = cut_two(rows_w[...].reshape(n_col * depth, rows_w.shape[2]))
        gram = dot3(right, tile_right, ((0,), (0,)))
        tile_left = tile[n_col:].reshape(-1, width)
        tile_left = cut_two(jnp.where(lane < column_rank, tile_left, 0.0))
        middle = dot3(cut_two(gram), tile_left, ((1,), (1,)))
        rhs = dot3(right, solved, ((0,), (0,)))
        middle = jnp.where(sub < rank, middle, 0.0)
        rhs = jnp.where(sub < rank, rhs, 0.0)
        rows = middle.shape[1]
        mid_high[:, :rows], mid_low[:, :rows] = cut_two(middle)
        mid_high[:, rows:], mid_low[:, rows:] = cut_two(rhs)

    left = cut_two(rows_l[0])
    update = dot3(left, (mid_high[...], mid_low[...]), ((1,), (0,)))
    rows = trailing.shape[1]
    trail_out[...] = trailing[...] - update[:, :rows]
    rhs_out[...] = sides_in[...] - update[:, rows:]


def update(order, ranks, rows_l, rows_r, tile, rows_w, trailing, right_sides):
    slots, width = rows_r.shape[0], rows_r.shape[3]
    rows, columns = trailing.shape
    others = right_sides.shape[1]
    blocks = 2
    size = rows // slots // blocks
    rows_l = rows_l.reshape(slots * blocks, size, width)
    smem = pl.BlockSpec(memory_space=pltpu.SMEM)
    vmem = pl.BlockSpec(memory_space=pltpu.VMEM)

    def place(s, i):
        return (s * blocks + i, 0)

    return pl.pallas_call(
        update_kernel,
        grid=(slots, blocks),
        out_shape=(jax.ShapeDtypeStruct(trailing.shape, jnp.float32), jax.ShapeDtypeStruct(right_sides.shape, jnp.float32)),
        in_specs=[
            smem,
            smem,
            pl.BlockSpec((1, size, width), lambda s, i: (s * blocks + i, 0, 0)),
            vmem,
            vmem,
            vmem,
            pl.BlockSpec((size, columns), place),
            pl.BlockSpec((size, others), place),
        ],
        out_specs=(pl.BlockSpec((size, columns), place), pl.BlockSpec((size, others), place)),
        scratch_shapes=[pltpu.VMEM((width, columns + others), jnp.bfloat16)] * 2,
        compiler_params=pltpu.CompilerParams(vmem_limit_bytes=28 * 1024 * 1024),
        name="update_panel",
    )(order, ranks, rows_l, rows_r, tile, rows_w, trailing, right_sides)


def on_device(n_row, n_col, trailing, panel_left, panel_right, panel_solved, right_sides, tile_ranks, tile_order):
    rows_l, rows_r, tile, rows_w = gather(n_row, n_col, tile_order, panel_left, panel_right, panel_solved)
    return update(tile_order, tile_ranks, rows_l, rows_r, tile, rows_w, trailing, right_sides)


def solution(mesh):
    return jax.shard_map(
        functools.partial(on_device, mesh.shape["row"], mesh.shape["col"]),
        mesh=mesh,
        in_specs=(
            P("row", "col"),
            P(("row", "col"), None),
            P("row", "col", None),
            P("row", "col"),
            P("row", "col"),
            P(),
            P(),
        ),
        out_specs=(P("row", "col"), P("row", "col")),
        check_vma=False,
    )
```

time: 90.3 us -> 92.8 us (1.028)
  Pallas kernels: 71.4 us -> 85.1 us
  matrix products: 6.77 us -> 0 us
  other arithmetic: 6.35 us -> 0 us
  local copies, waits for them, and re-layouts: 4.75 us -> 6.76 us
    pallas_call x0 -> x1, Pallas kernels: none -> 12.2 us  [update(): pl.pallas_call(update_kernel, grid=(slots, blocks), out_shape=(jax.ShapeD...]
    dot_general x3 -> x0, matrix products: 6.77 us -> none  [high(): jnp.einsum(spec, a, b, precision=lax.Precision.HIGH, preferred_element_ty...]
    reduce_sum x3 -> x0, other arithmetic: 2.99 us -> none  [the longest x1 1.31 us: on_device(): root = jnp.sum(jnp.where(tile_order == column, places, 0)).astype(jnp.int32)]
    sub x2 -> x0, other arithmetic: 2.47 us -> none  [the longest x1 1.62 us: on_device(): trailing - update[:, :tile_rows]]
    unnamed x12 -> x14, local copies, waits for them, and re-layouts: 4.54 us -> 6.76 us
    pallas_call x1, Pallas kernels: 71.4 us -> 72.9 us  [gather(): pl.pallas_call(functools.partial(gather_kernel, n_row, n_col, slots), out...]
where the time goes in v2:
time: 92.8 us; the launch traced here: 92.5 us
  Pallas kernels  85.1 us (92%)
  local copies, waits for them, and re-layouts  6.76 us (7%)
    pallas_call x1, Pallas kernels, gather(): pl.pallas_call(functools.partial(gather_kernel, n_row, n_col, slots), out...  72.9 us
    pallas_call x1, Pallas kernels, update(): pl.pallas_call(update_kernel, grid=(slots, blocks), out_shape=(jax.ShapeD...  12.2 us
    unnamed x14, local copies, waits for them, and re-layouts  6.76 us

profile of v2, /device:TPU:0, one launch (start us, length us, event | category | flops | bytes accessed | tf_op | source)
XLA Modules:
  0.0 92.5 jit_solution(16289678261837332451)
XLA Ops:
  0.6 0.0 copy-start.2
  0.6 1.0 %copy-done.2 = f32[2,128,384]{2,1,0:T(8,128)S(1)} copy-done((f32[2,128,384]{2,1,0:T(8,128)S(1)}, f32[2,128,384]{2,1,0:T(8,128)}, u32[]{:S(2)}) %copy-start.2) | copy-done | bytes 393240
  1.6 0.0 copy-start.3
  1.6 0.9 copy-done.3
  2.6 0.0 copy-start.4
  2.6 0.9 copy-done.4
  3.5 0.0 copy-start.5
  3.5 0.7 copy-done.5
  4.1 72.9 %gather_panel.1 = (f32[8,128,384]{2,1,0:T(8,128)S(1)}, f32[2,8,128,384]{3,2,1,0:T(8,128)S(1)}, f32[12,128,384]{2,1,0:T(8,128)S(1)}, f32[4,256,128]{2,1,0:T(8,128)S(1)}) custom-call(s32[8]{0:T(128)S(1)} %copy-done.5, f32[128,384]{1,0:T(8,128)S(1)} %copy-done.3, f32[2,128,384]{2,1,0:T(8,128)S(1)} %copy-done.2, f32[256,128]{1,0:T(8,128)S(1)} %copy-done.4), custom_call_target="tpu_custom_call" | custom-call | tf_op jit(solution)/shard_map/gather_panel/pallas_call | solution.py:286
  77.0 0.0 copy-start
  77.1 1.6 %copy-done = f32[1024,512]{1,0:T(8,128)S(1)} copy-done((f32[1024,512]{1,0:T(8,128)S(1)}, f32[1024,512]{1,0:T(8,128)}, u32[]{:S(2)}) %copy-start) | copy-done | bytes 2097176
  78.6 0.0 copy-start.1
  78.6 1.0 %copy-done.1 = f32[1024,128]{1,0:T(8,128)S(1)} copy-done((f32[1024,128]{1,0:T(8,128)S(1)}, f32[1024,128]{1,0:T(8,128)}, u32[]{:S(2)}) %copy-start.1) | copy-done | bytes 524312
  79.7 0.0 copy-start.6
  79.7 0.7 copy-done.6
  80.3 12.2 %update_panel.1 = (f32[1024,512]{1,0:T(8,128)}, f32[1024,128]{1,0:T(8,128)}) custom-call(s32[8]{0:T(128)S(1)} %copy-done.5, s32[8]{0:T(128)S(1)} %copy-done.6, f32[4,256,384]{2,1,0:T(8,128)S(1)} %bitcast.1, f32[2,8,128,384]{3,2,1,0:T(8,128)S(1)} %get-tuple-element.7.rows_r, f32[12,128,384]{2,1,0:T(8,128)S(1)} %get-tuple-element.8.tile, ...), custom_call_target="tpu_custom_call" | custom-call | tf_op jit(solution)/shard_map/update_panel/pallas_call | solution.py:380
Async XLA Ops:
  0.6 1.0 %copy-start.2 = (f32[2,128,384]{2,1,0:T(8,128)S(1)}, f32[2,128,384]{2,1,0:T(8,128)}, u32[]{:S(2)}) copy-start(f32[2,128,384]{2,1,0:T(8,128)} %right.1) | copy-start | bytes 1179652
  1.6 0.9 %copy-start.3 = (f32[128,384]{1,0:T(8,128)S(1)}, f32[128,384]{1,0:T(8,128)}, u32[]{:S(2)}) copy-start(f32[128,384]{1,0:T(8,128)} %left.1) | copy-start | bytes 589828
  2.6 0.9 copy-start.4
  3.5 0.7 copy-start.5
  77.0 1.6 %copy-start = (f32[1024,512]{1,0:T(8,128)S(1)}, f32[1024,512]{1,0:T(8,128)}, u32[]{:S(2)}) copy-start(f32[1024,512]{1,0:T(8,128)} %trailing.1) | copy-start | bytes 6291460
  78.6 1.0 %copy-start.1 = (f32[1024,128]{1,0:T(8,128)S(1)}, f32[1024,128]{1,0:T(8,128)}, u32[]{:S(2)}) copy-start(f32[1024,128]{1,0:T(8,128)} %sides_in.1) | copy-start | bytes 1572868
  79.7 0.7 copy-start.6

commit v3 on v2

--- a/solution.py
+++ b/solution.py
@@ -16,7 +16,7 @@
     for side in range(2):
         src = z - d if side == 0 else z + d
         ok = src >= 0 if side == 0 else (src < length) & (d > 0)
-        pl.when(ok)(functools.partial(body, src, side))
+        pl.when(ok & (d >= 0))(functools.partial(body, src, side))
 
 
 def find(order, value):
@@ -26,8 +26,8 @@
     return place
 
 
-def gather_kernel(n_row, n_col, slots, order, left, right, solved, rows_l, rows_r, tile, rows_w,
-                  first_out, first_in, chip, far_in, own_sem, rsem, zsem, ysem, fsem, frsem, xsem, xrsem, tsem, trsem, wsem, wrsem):
+def gather_kernel(n_row, n_col, slots, order, left, right, solved, rows_l, both_out, tile,
+                  rows_r, rows_w, first_out, first_in, chip, far_in, own_sem, rsem, zsem, ysem, fsem, frsem, xsem, xrsem, tsem, trsem, wsem, wrsem):
     length = n_col // ACROSS
     half = length // slots
     teams = n_row // CORES
@@ -160,7 +160,6 @@
         lax.fori_loop(0, half, one, 0)
 
     def far(d, body):
-        lefts(d, body)
         sources(d, lambda src, side: body(src * ACROSS + 1 - y, False))
 
     def along(d, side, act):
@@ -172,8 +171,8 @@
         def _():
             act(1)
 
-    def forward(d):
-        for p in range(late):
+    def pass_on(d, pieces):
+        for p in pieces:
             def one(src, side, p=p):
                 @pl.when(d > 0)
                 def _():
@@ -184,6 +183,7 @@
 
             sources(d, one)
 
+    def pass_late(d):
         def both(src, side):
             @pl.when(d > 0)
             def _():
@@ -199,42 +199,72 @@
 
         sources(d, both)
 
-    def arrive(d):
+    def arrive(d, pieces):
         def one(src, side):
-            for p in range(late):
+            for p in pieces:
                 y_copy(p, src, src * ACROSS + 1 - y).wait_recv()
 
         sources(d, one)
 
-    def step(d, _):
-        @pl.when(d < length)
-        def _():
-            forward(d)
-            near(d, stage_one)
-
-        @pl.when(d == 0)
+    def w_wait():
+        for k in range(1, n_row):
+            w_copy(k).wait_send()
+            other = lax.rem(row + k, n_row)
+            ref = rows_w.at[other]
+            pltpu.make_async_remote_copy(ref, ref, wsem.at[k], wrsem.at[other], device_id=(other, col), device_id_type=MESH).wait_recv()
+
+    width = tile.shape[2]
+    depth = tile.shape[1]
+    per = n_col // n_row
+    both_out[...] = jnp.zeros_like(both_out)
+
+    def accumulate(t):
+        def one(c, _):
+            src = c // ACROSS
+            when = jnp.abs(z - src) + 2
+
+            @pl.when(when == t)
+            def _():
+                t_copy(c, 1 - core).wait_recv()
+                start = pl.multiple_of((c % per) * depth, depth)
+                others = cut_two(rows_w[c // per, pl.ds(start, depth)])
+                column = cut_two(tile[c])
+                for s in range(slots):
+                    mine = cut_two(rows_r[s, c])
+                    both_out[s, :, :width] += dot3(mine, column, ((0,), (0,)))
+                    both_out[s, :, width:] += dot3(mine, others, ((0,), (0,)))
+
+            return 0
+
+        lax.fori_loop(0, n_col, one, 0)
+
+    early = tuple(range(late))
+
+    def step(t, _):
+        pass_on(t, early)
+        pass_late(t)
+        near(t, stage_one)
+
+        @pl.when(t == 0)
         def _():
             for k in range(1, n_row):
                 w_copy(k).start()
 
-        @pl.when((d >= 1) & (d <= length))
+        arrive(t - 1, early)
+        lefts(t - 1, stage_one)
+        far(t - 1, stage_one)
+        near(t, stage_two)
+        lefts(t - 1, stage_two)
+        far(t - 1, stage_two)
+        near(t - 1, stage_three)
+        lefts(t - 2, stage_three)
+        far(t - 2, stage_three)
+
+        @pl.when(t == 2)
         def _():
-            arrive(d - 1)
-            far(d - 1, stage_one)
-
-        @pl.when(d < length)
-        def _():
-            near(d, stage_two)
-
-        @pl.when((d >= 1) & (d <= length))
-        def _():
-            far(d - 1, stage_two)
-            near(d - 1, stage_three)
-
-        @pl.when(d >= 2)
-        def _():
-            far(d - 2, stage_three)
-
+            w_wait()
+
+        accumulate(t)
         return 0
 
     lax.fori_loop(0, length + 2, step, 0)
@@ -262,14 +292,14 @@
         for k in range(1, teams):
             x_copy(c, k, team).wait_send()
         t_copy(c, core).wait_send()
-        t_copy(c, 1 - core).wait_recv()
+
+        @pl.when(c >= n_col)
+        def _():
+            t_copy(c, 1 - core).wait_recv()
+
         return 0
 
     lax.fori_loop(0, n_col + half * ACROSS, finish, 0)
-    for k in range(1, n_row):
-        w_copy(k).wait_send()
-        other = lax.rem(row + k, n_row)
-        pltpu.make_async_remote_copy(rows_w.at[other], rows_w.at[other], wsem.at[k], wrsem.at[other], device_id=(other, col), device_id_type=MESH).wait_recv()
 
 
 def gather(n_row, n_col, order, left, right, solved):
@@ -287,13 +317,14 @@
         functools.partial(gather_kernel, n_row, n_col, slots),
         out_shape=(
             jax.ShapeDtypeStruct((n_col,) + left.shape, f32),
-            jax.ShapeDtypeStruct((slots, n_col) + block, f32),
+            jax.ShapeDtypeStruct((slots, width, width + solved.shape[1]), f32),
             jax.ShapeDtypeStruct((chunks,) + block, f32),
-            jax.ShapeDtypeStruct((n_row,) + solved.shape, f32),
         ),
         in_specs=[pl.BlockSpec(memory_space=pltpu.SMEM), hbm, hbm, hbm],
-        out_specs=(vmem, vmem, vmem, vmem),
+        out_specs=(vmem, vmem, vmem),
         scratch_shapes=[
+            pltpu.VMEM((slots, n_col) + block, f32),
+            pltpu.VMEM((n_row,) + solved.shape, f32),
             pltpu.VMEM((chunks,) + part, f32),
             pltpu.VMEM((chunks,) + part, f32),
             pltpu.VMEM((chunks,) + part, f32),
@@ -311,7 +342,7 @@
             dma((n_row,)),
             dma((n_row,)),
         ],
-        compiler_params=pltpu.CompilerParams(collective_id=0, has_side_effects=True, vmem_limit_bytes=28 * 1024 * 1024),
+        compiler_params=pltpu.CompilerParams(collective_id=0, has_side_effects=True, vmem_limit_bytes=55 * 1024 * 1024),
         name="gather_panel",
     )(order, left, right, solved)
 
@@ -330,10 +361,8 @@
     return dot(ah, bh) + (dot(ah, bl) + dot(al, bh))
 
 
-def update_kernel(order, ranks, rows_l, rows_r, tile, rows_w, trailing, sides_in, trail_out, rhs_out, mid_high, mid_low):
-    slots = rows_r.shape[0]
-    n_col, depth, width = tile.shape
-    n_col = rows_r.shape[1]
+def update_kernel(order, ranks, rows_l, both, tile, trailing, sides_in, trail_out, rhs_out, mid_high, mid_low):
+    slots, width = both.shape[0], both.shape[1]
     slot, step = pl.program_id(0), pl.program_id(1)
 
     @pl.when(step == 0)
@@ -343,19 +372,13 @@
         column_rank = ranks[lax.axis_index("col")]
         lane = lax.broadcasted_iota(jnp.int32, (1, width), 1)
         sub = lax.broadcasted_iota(jnp.int32, (width, 1), 0)
-        right = cut_two(rows_r[slot].reshape(n_col * depth, width))
-        tile_right = cut_two(tile[:n_col].reshape(n_col * depth, width))
-        solved = cut_two(rows_w[...].reshape(n_col * depth, rows_w.shape[2]))
-        gram = dot3(right, tile_right, ((0,), (0,)))
-        tile_left = tile[n_col:].reshape(-1, width)
+        tile_left = tile[...].reshape(-1, width)
         tile_left = cut_two(jnp.where(lane < column_rank, tile_left, 0.0))
-        middle = dot3(cut_two(gram), tile_left, ((1,), (1,)))
-        rhs = dot3(right, solved, ((0,), (0,)))
-        middle = jnp.where(sub < rank, middle, 0.0)
-        rhs = jnp.where(sub < rank, rhs, 0.0)
+        gram = cut_two(jnp.where(sub < rank, both[slot, :, :width], 0.0))
+        middle = dot3(gram, tile_left, ((1,), (1,)))
         rows = middle.shape[1]
         mid_high[:, :rows], mid_low[:, :rows] = cut_two(middle)
-        mid_high[:, rows:], mid_low[:, rows:] = cut_two(rhs)
+        mid_high[:, rows:], mid_low[:, rows:] = cut_two(jnp.where(sub < rank, both[slot, :, width:], 0.0))
 
     left = cut_two(rows_l[0])
     update = dot3(left, (mid_high[...], mid_low[...]), ((1,), (0,)))
@@ -364,13 +387,15 @@
     rhs_out[...] = sides_in[...] - update[:, rows:]
 
 
-def update(order, ranks, rows_l, rows_r, tile, rows_w, trailing, right_sides):
-    slots, width = rows_r.shape[0], rows_r.shape[3]
+def update(order, ranks, rows_l, both, tile, trailing, right_sides):
+    slots, width = both.shape[0], both.shape[1]
     rows, columns = trailing.shape
     others = right_sides.shape[1]
     blocks = 2
     size = rows // slots // blocks
     rows_l = rows_l.reshape(slots * blocks, size, width)
+    chunks, depth = tile.shape[0], tile.shape[1]
+    lefts = columns // depth
     smem = pl.BlockSpec(memory_space=pltpu.SMEM)
     vmem = pl.BlockSpec(memory_space=pltpu.VMEM)
 
@@ -386,21 +411,20 @@
             smem,
             pl.BlockSpec((1, size, width), lambda s, i: (s * blocks + i, 0, 0)),
             vmem,
-            vmem,
-            vmem,
+            pl.BlockSpec((lefts, depth, width), lambda s, i: (chunks // lefts - 1, 0, 0)),
             pl.BlockSpec((size, columns), place),
             pl.BlockSpec((size, others), place),
         ],
         out_specs=(pl.BlockSpec((size, columns), place), pl.BlockSpec((size, others), place)),
         scratch_shapes=[pltpu.VMEM((width, columns + others), jnp.bfloat16)] * 2,
-        compiler_params=pltpu.CompilerParams(vmem_limit_bytes=28 * 1024 * 1024),
+        compiler_params=pltpu.CompilerParams(vmem_limit_bytes=55 * 1024 * 1024),
         name="update_panel",
-    )(order, ranks, rows_l, rows_r, tile, rows_w, trailing, right_sides)
+    )(order, ranks, rows_l, both, tile, trailing, right_sides)
 
 
 def on_device(n_row, n_col, trailing, panel_left, panel_right, panel_solved, right_sides, tile_ranks, tile_order):
-    rows_l, rows_r, tile, rows_w = gather(n_row, n_col, tile_order, panel_left, panel_right, panel_solved)
-    return update(tile_order, tile_ranks, rows_l, rows_r, tile, rows_w, trailing, right_sides)
+    rows_l, both, tile = gather(n_row, n_col, tile_order, panel_left, panel_right, panel_solved)
+    return update(tile_order, tile_ranks, rows_l, both, tile, trailing, right_sides)
 
 
 def solution(mesh):

time: 92.8 us -> 85.8 us (0.925)
  local copies, waits for them, and re-layouts: 6.76 us -> 0 us
    unnamed x14 -> x0, local copies, waits for them, and re-layouts: 6.76 us -> none
    pallas_call x1, Pallas kernels: 12.2 us -> 8.28 us  [update(): pl.pallas_call(update_kernel, grid=(slots, blocks), out_shape=(jax.ShapeD...]
    pallas_call x1, Pallas kernels: 72.9 us -> 76.7 us  [gather(): pl.pallas_call(functools.partial(gather_kernel, n_row, n_col, slots), out...]
where the time goes in v3:
time: 85.8 us; the launch traced here: 85.6 us
  Pallas kernels  85 us (99%)
    pallas_call x1, Pallas kernels, gather(): pl.pallas_call(functools.partial(gather_kernel, n_row, n_col, slots), out...  76.7 us
    pallas_call x1, Pallas kernels, update(): pl.pallas_call(update_kernel, grid=(slots, blocks), out_shape=(jax.ShapeD...  8.28 us

profile of v3, /device:TPU:0, one launch (start us, length us, event | category | flops | bytes accessed | tf_op | source)
XLA Modules:
  0.0 85.6 jit_solution(9459960305942145653)
XLA Ops:
  0.6 76.7 %gather_panel.1 = (f32[8,128,384]{2,1,0:T(8,128)}, f32[2,384,512]{2,1,0:T(8,128)}, f32[12,128,384]{2,1,0:T(8,128)}) custom-call(s32[8]{0:T(128)} %order.3, f32[128,384]{1,0:T(8,128)} %left.1, f32[2,128,384]{2,1,0:T(8,128)} %right.1, f32[256,128]{1,0:T(8,128)} %solved.1), custom_call_target="tpu_custom_call" | custom-call | tf_op jit(solution)/shard_map/gather_panel/pallas_call | solution.py:316
  77.4 8.3 %update_panel.1 = (f32[1024,512]{1,0:T(8,128)}, f32[1024,128]{1,0:T(8,128)}) custom-call(s32[8]{0:T(128)} %order.3, s32[8]{0:T(128)} %ranks.1, f32[4,256,384]{2,1,0:T(8,128)} %bitcast.1, f32[2,384,512]{2,1,0:T(8,128)} %get-tuple-element.6.both, f32[12,128,384]{2,1,0:T(8,128)} %get-tuple-element.7.tile, f32[1024,512]{1,0:T(8,128)} %trailing.1, ...), custom_call_target="tpu_custom_call" | custom-call | tf_op jit(solution)/shard_map/update_panel/pallas_call | solution.py:405
